TPU v7x, 128 devices: a whole 4x4x4 slice. The times are simulated.
128 devices in a mesh: tile: 16 (over x_lo, z, core), chan: 8 (over y, x_hi).
Axes of the slice: x: 4 (x_hi: 2, x_lo: 2; x = x_hi * 2 + x_lo), y: 4, z: 4, core: 2. Of those that a mesh axis runs over, the one named last changes fastest.
Arguments:
- voltages: int32 [512, 262144], P('tile', 'chan'), may hold values from -128 to 127
- history: int32 [512, 30720], P('tile'), may hold values from -128 to 127
- filter_taps: int32 [16, 2048], replicated, may hold values from -64 to 64
Outputs:
- visibilities: float32 [2, 1024, 512, 512], P(None, 'chan', 'tile')
Inputs may be any that keep to these rules, and one draw needn't show every extreme that they name: `voltages`: 8-bit signed samples. `history`: 8-bit signed samples.
All inputs are finite; a program needn't handle non-finite values.
Results may differ from a plain program's by a relative error of at most 0.006.
Values may be sent and summed in bfloat16 or wider, within the bound.
A program may use at most 192 MiB of HBM per device.

v0:
```python
import math
import jax
import jax.numpy as jnp
from jax import lax
from jax.sharding import PartitionSpec as P

CH = 1024
TAPS = 16
FFT = 2048
filter_norm = 1.0 / 16384.0


def from_behind(value, axis, steps):
    count = lax.axis_size(axis)
    leading, last = (max(0, -steps), min(count, count - steps))
    return lax.ppermute(value, axis, [(source, source + steps) for source in range(leading, last)])


def dft_table(samples, channels):
    rows_index = jnp.arange(samples, dtype=jnp.int32)[:, None]
    cols_index = jnp.arange(channels, dtype=jnp.int32)[None, :]
    angles = (rows_index * cols_index % samples).astype(jnp.float32) * (2.0 * math.pi / samples)
    factor = 1.0 / math.sqrt(channels)
    return jnp.concatenate([jnp.cos(angles) * factor, -jnp.sin(angles) * factor], axis=1).astype(
        jnp.bfloat16
    )


def polyphase(extended, weights, spectra_count):
    summed = jnp.zeros((extended.shape[0], spectra_count, extended.shape[2]), jnp.float32)
    for tap_index in range(weights.shape[0]):
        summed = (
            summed
            + weights[tap_index][None, None, :]
            * extended[:, tap_index : tap_index + spectra_count, :]
        )
    return summed


def counter_rows(spectra):
    real_part = spectra[:, :, 0]
    imag_part = spectra[:, :, 1]
    rotated = jnp.stack([imag_part, -real_part], axis=2)
    return jnp.stack([spectra, rotated], axis=0)


def body(voltages, history, filter_taps):
    local_inputs = voltages.shape[0]
    spectra_count = voltages.shape[1] // FFT
    tail_blocks = voltages[:, (spectra_count - TAPS + 1) * FFT :].astype(jnp.bfloat16)
    carried = from_behind(tail_blocks, "chan", 1)
    is_first = lax.axis_index("chan") == 0
    earlier = jnp.where(is_first, history.astype(jnp.float32), carried.astype(jnp.float32))
    extended = jnp.concatenate([earlier, voltages.astype(jnp.float32)], axis=1)
    extended = extended.reshape(local_inputs, spectra_count + TAPS - 1, FFT)
    filtered = (
        polyphase(extended, filter_taps.astype(jnp.float32), spectra_count) * filter_norm
    ).astype(jnp.bfloat16)
    spectra = jnp.dot(
        filtered.reshape(-1, FFT), dft_table(FFT, CH), preferred_element_type=jnp.float32
    )
    spectra = spectra.reshape(local_inputs, spectra_count, 2, CH).astype(jnp.bfloat16)
    turned = lax.all_to_all(spectra, "chan", split_axis=3, concat_axis=1, tiled=True)
    total_spectra = turned.shape[1]
    average = 1.0 / total_spectra
    row_sets = counter_rows(turned)
    return (
        jnp.einsum(
            "qaspc,bspc->qcab",
            row_sets,
            lax.all_gather(turned, "tile", axis=0, tiled=True),
            preferred_element_type=jnp.float32,
        )
        * average
    )


def solution(mesh):
    in_specs = (P("tile", "chan"), P("tile", None), P())
    out_specs = P(None, "chan", "tile", None)
    return jax.shard_map(body, mesh=mesh, in_specs=in_specs, out_specs=out_specs, check_vma=False)
```

profile of v0, /device:TPU:1, one launch (start us, length us, event | category | flops | bytes accessed | tf_op | source)
XLA Modules:
  0.0 409.3 jit_solution(11984337973401259222)
XLA Ops:
  6.5 3.7 slice_convert_fusion
  10.3 5.6 %collective-permute-start = (bf16[32,30720]{1,0:T(8,128)(2,1)}, bf16[32,30720]{1,0:T(8,128)(2,1)S(1)}, u32[]{:S(2)}, u32[]{:S(2)}) collective-permute-start(bf16[32,30720]{1,0:T(8,128)(2,1)} %slice_convert_fusion), channel_id=1, source_target_pairs={{0,1},{1,2},{2,3},{3,4},{4,5},{5,6},{6,7},{8,9},{9,10},{10,11},{11... | collective-permute-start | bytes 5898248 | tf_op jit(solution)/shard_map/ppermute | solution.py:16
  15.9 0.1 fusion.40
  16.0 2.2 convert_element_type.28
  18.2 34.9 %multiply_convert_fusion = (bf16[2048,1024]{0,1:T(8,128)(2,1)}, bf16[2048,1024]{0,1:T(8,128)(2,1)}) fusion(), kind=kLoop, calls=%fused_computation.11 | loop fusion | flops 39845888 | bytes 8388608 | tf_op jit(solution)/shard_map/convert.1
  53.2 8.5 %pad_maximum_fusion = bf16[2048,2048]{0,1:T(8,128)(2,1)} fusion(bf16[2048,1024]{0,1:T(8,128)(2,1)} %get-tuple-element.23, bf16[2048,1024]{0,1:T(8,128)(2,1)} %get-tuple-element.24), kind=kLoop, calls=%fused_computation.10 | loop fusion | flops 16777216 | bytes 16777216 | tf_op jit(solution)/shard_map/concatenate | solution.py:24
  61.7 2.6 convert_select_fusion
  64.4 0.7 copy-done
  65.1 3.7 pad_maximum_fusion.1
  68.7 7.6 %reshape.25 = f32[32,31,2048]{2,1,0:T(8,128)} reshape(f32[32,63488]{1,0:T(8,128)} %pad_maximum_fusion.1) | data formatting | bytes 16252928 | tf_op jit(solution)/shard_map/reshape | solution.py:55
  76.4 43.5 %fusion.34 = bf16[32,16,2,1024]{3,1,2,0:T(8,128)(2,1)S(1)} fusion(bf16[2,1024,2048,1]{2,1,0,3:T(8,128)(2,1)} %bitcast.59, f32[32,31,2048]{2,1,0:T(8,128)} %reshape.25, f32[2048]{0:T(1024)S(1)} %bitcast.61, f32[2048]{0:T(1024)S(1)} %bitcast.62, f32[2048]{0:T(1024)S(1)} %bitcast.63, f32[2048]{0:T(1024)S(1)} %bitcast.64, f32[2048]{0:T(1024)S(1)} %bitcast.65, ...), kind=kOutput, calls=%fused_computation.58 | convolution fusion | flops 4330618880 | bytes 77725696 | tf_op jit(solution)/shard_map/dot_general | solution.py:59
  119.9 12.8 %copy.28 = bf16[32,16,2,1024]{0,1,2,3:T(8,128)(2,1)} copy(bf16[32,16,2,1024]{3,1,2,0:T(8,128)(2,1)S(1)} %fusion.34) | data formatting | bytes 4194304 | tf_op jit(solution)/shard_map/convert_element_type | solution.py:62
  132.7 10.1 %reshape.30 = bf16[8,2,65536]{2,1,0:T(2,128)(2,1)S(1)} reshape(bf16[1024,2,16,32]{3,2,1,0:T(8,128)(2,1)} %bitcast.55) | data formatting | bytes 4194304
  142.9 31.9 %all_to_all.18 = bf16[8,2,65536]{2,1,0:T(2,128)(2,1)} all-to-all(bf16[8,2,65536]{2,1,0:T(2,128)(2,1)S(1)} %reshape.30), channel_id=1, replica_groups=mesh['tile'=16,'chan'=8] {'chan'}, dimensions={0} | all-to-all | bytes 4194304 | tf_op jit(solution)/shard_map/all_to_all | solution.py:63
  174.8 8.6 %reshape.31 = bf16[1024,2,16,32]{3,2,1,0:T(8,128)(2,1)} reshape(bf16[8,2,65536]{2,1,0:T(2,128)(2,1)} %all_to_all.18) | data formatting | bytes 4194304
  183.4 10.3 %copy.30 = bf16[32,8,16,2,128]{4,2,1,3,0:T(8,128)(2,1)S(1)} copy(bf16[32,8,16,2,128]{0,2,3,4,1:T(8,128)(2,1)} %bitcast.56) | data formatting | bytes 4194304 | tf_op jit(solution)/shard_map/all_to_all | solution.py:63
  193.7 2.9 copy.31
  196.6 0.0 all-gather.2.cloned.1.call-update
  196.6 3.0 copy.35
  199.6 1.9 fusion.39
  201.5 1.5 maximum_bitcast_fusion
  203.1 165.1 %all-gather.2.cloned.1.call-done = bf16[512,128,2,128]{1,0,2,3:T(8,128)(2,1)} async-done(((bf16[32,128,2,128]{1,0,2,3:T(8,128)(2,1)}), bf16[512,128,2,128]{1,0,2,3:T(8,128)(2,1)}) %all-gather.2.cloned.1.call-update) | async-done | bytes 33554448 | tf_op jit(solution)/shard_map/all_gather | solution.py:71
  368.1 21.9 %fusion.2 = f32[2,128,32,512]{3,2,0,1:T(8,128)} fusion(bf16[512,128,2,128]{1,0,2,3:T(8,128)(2,1)} %all-gather.2.cloned.1.call-done, bf16[1,32,128,2,128]{2,1,3,0,4:T(8,128)(2,1)} %maximum_bitcast_fusion, bf16[1,32,128,2,128]{2,1,3,0,4:T(8,128)(2,1)S(1)} %copy-done.2), kind=kOutput, calls=%fused_computation.3 | convolution fusion | flops 2160066560 | bytes 54525952 | tf_op jit(solution)/shard_map/qaspc,bspc->qcab/dot_general | solution.py:68
  390.1 12.4 %copy.36 = f32[2,128,32,512]{3,2,1,0:T(8,128)} copy(f32[2,128,32,512]{3,2,0,1:T(8,128)} %fusion.2) | data formatting | bytes 33554432 | tf_op jit(solution)/shard_map/mul | solution.py:68
  (10 shorter events, 0.0 us)
Async XLA Ops:
  6.5 9.3 %copy-start.3 = (s32[16,2048]{1,0:T(8,128)S(1)}, s32[16,2048]{1,0:T(8,128)}, u32[]{:S(2)}) copy-start(s32[16,2048]{1,0:T(8,128)} %param.5) | copy-start | bytes 393220
  6.5 361.6 %all-gather.2.cloned.1.call-start = ((), (), s32[]{:S(2)}) async-start(), calls=%async_computation.1 | async-start | bytes 35651584 | tf_op jit(solution)/shard_map/all_gather | solution.py:71
  6.5 9.5 %copy-start.1 = (s32[32,32768]{1,0:T(8,128)S(1)}, s32[32,32768]{1,0:T(8,128)}, u32[]{:S(2)}) copy-start(s32[32,32768]{1,0:T(8,128)} %param.3) | copy-start | bytes 12582916
  10.3 51.4 %collective-permute-start = (bf16[32,30720]{1,0:T(8,128)(2,1)}, bf16[32,30720]{1,0:T(8,128)(2,1)S(1)}, u32[]{:S(2)}, u32[]{:S(2)}) collective-permute-start(bf16[32,30720]{1,0:T(8,128)(2,1)} %slice_convert_fusion), channel_id=1, source_target_pairs={{0,1},{1,2},{2,3},{3,4},{4,5},{5,6},{6,7},{8,9},{9,10},{10,11},{11... | collective-permute-start | bytes 5898248 | tf_op jit(solution)/shard_map/ppermute | solution.py:16
  61.7 3.4 copy-start
  199.6 168.5 %copy-start.2 = (bf16[1,32,128,2,128]{2,1,3,0,4:T(8,128)(2,1)S(1)}, bf16[1,32,128,2,128]{2,1,3,0,4:T(8,128)(2,1)}, u32[]{:S(2)}) copy-start(bf16[1,32,128,2,128]{2,1,3,0,4:T(8,128)(2,1)} %copy.35) | copy-start | bytes 6291460
Sparse Core Ops, SparseCore 0:
  196.8 171.3 all-gather.1
where the time goes:
time: 410 us; the launch traced here: 409 us
  waiting for transfers between devices  165 us (40%)
  local copies, waits for them, and re-layouts  68.6 us (17%)
  matrix products  65.5 us (16%)
  other arithmetic  59.2 us (14%)
  blocking collectives  31.9 us (8%)
  between operations  13.5 us (3%)
  starting transfers between devices  5.58 us (1%)
    all_gather x1, waiting for transfers between devices, body(): lax.all_gather(turned, 'tile', axis=0, tiled=True)  165 us
    dot_general x1, matrix products, body(): jnp.dot(filtered.reshape(-1, FFT), dft_table(FFT, CH), preferred_element_...  43.5 us
    another operation x2, other arithmetic  38.7 us
    all_to_all x1, blocking collectives, body(): lax.all_to_all(spectra, 'chan', split_axis=3, concat_axis=1, tiled=True)  31.9 us
    dot_general x1, matrix products, body(): jnp.einsum('qaspc,bspc->qcab', row_sets, lax.all_gather(turned, 'tile', a...  21.9 us
    unnamed x10, local copies, waits for them, and re-layouts  19.5 us
    all_to_all x2, local copies, waits for them, and re-layouts, body(): lax.all_to_all(spectra, 'chan', split_axis=3, concat_axis=1, tiled=True)  13.2 us
    convert_element_type x1, local copies, waits for them, and re-layouts, body(): spectra.reshape(local_inputs, spectra_count, 2, CH).astype(jnp.bfloat16)  12.8 us
  transfers between devices with their start and end apart: 2, of which 1 were waited for; matrix products, arithmetic and copies ran while one was open for 13% of the time, Pallas kernels for 0%

commit v1 on v0

--- a/solution.py
+++ b/solution.py
@@ -68,7 +68,9 @@
         jnp.einsum(
             "qaspc,bspc->qcab",
             row_sets,
-            lax.all_gather(turned, "tile", axis=0, tiled=True),
+            jnp.concatenate(
+                lax.all_to_all(jnp.stack([turned] * lax.axis_size("tile")), "tile", 0, 0), axis=0
+            ),
             preferred_element_type=jnp.float32,
         )
         * average

time: 410 us -> 793 us (1.93)
  waiting for transfers between devices: 165 us -> 519 us
  local copies, waits for them, and re-layouts: 68.6 us -> 106 us
  between operations: 13.5 us -> 0.09 us
  starting transfers between devices: 5.58 us -> 13.9 us
    all_to_all x0 -> x1, waiting for transfers between devices: none -> 519 us  [body(): lax.all_to_all(jnp.stack([turned] * lax.axis_size('tile')), 'tile', 0, 0)]
    all_gather x1 -> x0, waiting for transfers between devices: 165 us -> none  [body(): lax.all_gather(turned, 'tile', axis=0, tiled=True)]
    all_to_all x0 -> x1, local copies, waits for them, and re-layouts: none -> 23.1 us  [body(): lax.all_to_all(jnp.stack([turned] * lax.axis_size('tile')), 'tile', 0, 0)]
    another operation x1 -> x3, local copies, waits for them, and re-layouts: 2.97 us -> 19.5 us  [body(): jnp.stack([turned] * lax.axis_size('tile'))]
    all_to_all x0 -> x1, starting transfers between devices: none -> 8.34 us  [body(): lax.all_to_all(jnp.stack([turned] * lax.axis_size('tile')), 'tile', 0, 0)]
  transfers between devices with their start and end apart: 2 -> 2, of which waited for: 1 -> 1; matrix products, arithmetic and copies ran while one was open for 13% -> 7% of each run, Pallas kernels for 0% -> 0%
where the time goes in v1:
time: 793 us; the launch traced here: 792 us
  waiting for transfers between devices  519 us (65%)
  local copies, waits for them, and re-layouts  106 us (13%)
  matrix products  63.3 us (8%)
  other arithmetic  57.5 us (7%)
  blocking collectives  31.9 us (4%)
  starting transfers between devices  13.9 us (2%)
    all_to_all x1, waiting for transfers between devices, body(): lax.all_to_all(jnp.stack([turned] * lax.axis_size('tile')), 'tile', 0, 0)  519 us
    dot_general x1, matrix products, body(): jnp.dot(filtered.reshape(-1, FFT), dft_table(FFT, CH), preferred_element_...  41.3 us
    another operation x2, other arithmetic  38.7 us
    all_to_all x1, blocking collectives, body(): lax.all_to_all(spectra, 'chan', split_axis=3, concat_axis=1, tiled=True)  31.9 us
    all_to_all x1, local copies, waits for them, and re-layouts, body(): lax.all_to_all(jnp.stack([turned] * lax.axis_size('tile')), 'tile', 0, 0)  23.1 us
    dot_general x1, matrix products, body(): jnp.einsum('qaspc,bspc->qcab', row_sets, jnp.concatenate(lax.all_to_all(j...  22 us
    another operation x3, local copies, waits for them, and re-layouts, body(): jnp.stack([turned] * lax.axis_size('tile'))  19.5 us
    unnamed x10, local copies, waits for them, and re-layouts  19.5 us
  transfers between devices with their start and end apart: 2, of which 1 were waited for; matrix products, arithmetic and copies ran while one was open for 7% of the time, Pallas kernels for 0%

profile of v1, /device:TPU:1, one launch (start us, length us, event | category | flops | bytes accessed | tf_op | source)
XLA Modules:
  0.0 791.7 jit_solution(9043852639359704026)
XLA Ops:
  0.0 3.8 slice_convert_fusion
  3.8 5.6 collective-permute-start
  9.5 2.2 convert_element_type.28
  11.7 34.9 %multiply_convert_fusion = (bf16[2048,1024]{0,1:T(8,128)(2,1)}, bf16[2048,1024]{0,1:T(8,128)(2,1)}) fusion(), kind=kLoop, calls=%fused_computation.9 | loop fusion | flops 39845888 | bytes 8388608 | tf_op jit(solution)/shard_map/convert.1
  46.6 8.5 %pad_maximum_fusion = bf16[2048,2048]{0,1:T(8,128)(2,1)} fusion(bf16[2048,1024]{0,1:T(8,128)(2,1)} %get-tuple-element.23, bf16[2048,1024]{0,1:T(8,128)(2,1)} %get-tuple-element.24), kind=kLoop, calls=%fused_computation.8 | loop fusion | flops 16777216 | bytes 16777216 | tf_op jit(solution)/shard_map/concatenate | solution.py:24
  55.2 2.6 convert_select_fusion
  57.8 0.7 copy-done
  58.5 3.7 pad_maximum_fusion.1
  62.2 7.6 reshape.30
  69.8 41.3 %fusion.30 = bf16[32,16,2,1024]{3,1,2,0:T(8,128)(2,1)S(1)} fusion(bf16[2,1024,2048,1]{2,1,0,3:T(8,128)(2,1)} %bitcast.59, f32[32,31,2048]{2,1,0:T(8,128)} %reshape.30, f32[2048]{0:T(1024)S(1)} %bitcast.61, f32[2048]{0:T(1024)S(1)} %bitcast.62, f32[2048]{0:T(1024)S(1)} %bitcast.63, f32[2048]{0:T(1024)S(1)} %bitcast.64, f32[2048]{0:T(1024)S(1)} %bitcast.65, ...), kind=kOutput, calls=%fused_computation.56 | convolution fusion | flops 4330618880 | bytes 77725696 | tf_op jit(solution)/shard_map/dot_general | solution.py:59
  111.2 12.8 %copy.30 = bf16[32,16,2,1024]{0,1,2,3:T(8,128)(2,1)} copy(bf16[32,16,2,1024]{3,1,2,0:T(8,128)(2,1)S(1)} %fusion.30) | data formatting | bytes 4194304 | tf_op jit(solution)/shard_map/convert_element_type | solution.py:62
  124.0 10.1 %reshape.36 = bf16[8,2,65536]{2,1,0:T(2,128)(2,1)S(1)} reshape(bf16[1024,2,16,32]{3,2,1,0:T(8,128)(2,1)} %bitcast.55) | data formatting | bytes 4194304
  134.2 31.9 %all_to_all.20 = bf16[8,2,65536]{2,1,0:T(2,128)(2,1)} all-to-all(bf16[8,2,65536]{2,1,0:T(2,128)(2,1)S(1)} %reshape.36), channel_id=1, replica_groups=mesh['tile'=16,'chan'=8] {'chan'}, dimensions={0} | all-to-all | bytes 4194304 | tf_op jit(solution)/shard_map/all_to_all | solution.py:63
  166.1 8.6 %reshape.37 = bf16[1024,2,16,32]{3,2,1,0:T(8,128)(2,1)} reshape(bf16[8,2,65536]{2,1,0:T(2,128)(2,1)} %all_to_all.20) | data formatting | bytes 4194304
  174.7 11.3 %copy.32 = bf16[32,8,16,2,128]{4,2,1,3,0:T(8,128)(2,1)} copy(bf16[32,8,16,2,128]{0,2,3,4,1:T(8,128)(2,1)} %bitcast.56) | data formatting | bytes 4194304 | tf_op jit(solution)/shard_map/all_to_all | solution.py:63
  186.0 3.5 copy.33
  189.5 11.4 %stack.13 = bf16[16,32,128,2,128]{2,1,3,4,0:T(8,128)(2,1)} broadcast(bf16[32,128,2,128]{1,0,2,3:T(8,128)(2,1)S(1)} %copy.33), dimensions={1,2,3,4} | broadcast | bytes 35651584 | tf_op jit(solution)/shard_map/stack | solution.py:72
  200.9 8.3 %all-to-all-start.1 = ((bf16[16,32,128,2,128]{2,1,3,4,0:T(8,128)(2,1)}), bf16[16,32,128,2,128]{2,1,3,4,0:T(8,128)(2,1)}, u32[]{:S(2)}, u32[]{:S(2)}) async-start(bf16[16,32,128,2,128]{2,1,3,4,0:T(8,128)(2,1)} %stack.13), calls=%async_computation.1 | async-start | bytes 67108864 | tf_op jit(solution)/shard_map/all_to_all | solution.py:72
  209.2 4.6 copy.38
  214.0 1.5 maximum_bitcast_fusion
  215.5 518.6 %all-to-all-done.1 = bf16[16,32,128,2,128]{2,1,3,4,0:T(8,128)(2,1)} async-done(((bf16[16,32,128,2,128]{2,1,3,4,0:T(8,128)(2,1)}), bf16[16,32,128,2,128]{2,1,3,4,0:T(8,128)(2,1)}, u32[]{:S(2)}, u32[]{:S(2)}) %all-to-all-start.1) | async-done | bytes 33554464 | tf_op jit(solution)/shard_map/all_to_all | solution.py:72
  734.2 23.1 %copy.34 = bf16[16,32,128,2,128]{2,1,0,3,4:T(8,128)(2,1)} copy(bf16[16,32,128,2,128]{2,1,3,4,0:T(8,128)(2,1)} %all-to-all-done.1) | data formatting | bytes 67108864 | tf_op jit(solution)/shard_map/all_to_all | solution.py:72
  757.3 22.0 %fusion = f32[2,128,32,512]{3,2,0,1:T(8,128)} fusion(bf16[512,128,2,128,1]{1,0,2,4,3:T(8,128)(2,1)} %bitcast.54, bf16[1,32,128,2,128]{2,1,3,0,4:T(8,128)(2,1)} %maximum_bitcast_fusion, bf16[1,32,128,2,128]{2,1,3,0,4:T(8,128)(2,1)S(1)} %copy-done.2), kind=kOutput, calls=%fused_computation.1 | convolution fusion | flops 2160066560 | bytes 54525952 | tf_op jit(solution)/shard_map/qaspc,bspc->qcab/dot_general | solution.py:68
  779.3 12.4 %copy.39 = f32[2,128,32,512]{3,2,1,0:T(8,128)} copy(f32[2,128,32,512]{3,2,0,1:T(8,128)} %fusion) | data formatting | bytes 33554432 | tf_op jit(solution)/shard_map/mul | solution.py:68
  (11 shorter events, 0.3 us)
Async XLA Ops:
  0.0 9.5 %copy-start.1 = (s32[32,32768]{1,0:T(8,128)S(1)}, s32[32,32768]{1,0:T(8,128)}, u32[]{:S(2)}) copy-start(s32[32,32768]{1,0:T(8,128)} %param.3) | copy-start | bytes 12582916
  0.0 9.3 %copy-start.3 = (s32[16,2048]{1,0:T(8,128)S(1)}, s32[16,2048]{1,0:T(8,128)}, u32[]{:S(2)}) copy-start(s32[16,2048]{1,0:T(8,128)} %param.5) | copy-start | bytes 393220
  3.8 51.4 %collective-permute-start = (bf16[32,30720]{1,0:T(8,128)(2,1)}, bf16[32,30720]{1,0:T(8,128)(2,1)S(1)}, u32[]{:S(2)}, u32[]{:S(2)}) collective-permute-start(bf16[32,30720]{1,0:T(8,128)(2,1)} %slice_convert_fusion), channel_id=1, source_target_pairs={{0,1},{1,2},{2,3},{3,4},{4,5},{5,6},{6,7},{8,9},{9,10},{10,11},{11... | collective-permute-start | bytes 5898248 | tf_op jit(solution)/shard_map/ppermute | solution.py:16
  55.2 3.4 copy-start
  200.9 533.3 %all-to-all-start.1 = ((bf16[16,32,128,2,128]{2,1,3,4,0:T(8,128)(2,1)}), bf16[16,32,128,2,128]{2,1,3,4,0:T(8,128)(2,1)}, u32[]{:S(2)}, u32[]{:S(2)}) async-start(bf16[16,32,128,2,128]{2,1,3,4,0:T(8,128)(2,1)} %stack.13), calls=%async_computation.1 | async-start | bytes 67108864 | tf_op jit(solution)/shard_map/all_to_all | solution.py:72
  215.5 541.7 %copy-start.2 = (bf16[1,32,128,2,128]{2,1,3,0,4:T(8,128)(2,1)S(1)}, bf16[1,32,128,2,128]{2,1,3,0,4:T(8,128)(2,1)}, u32[]{:S(2)}) copy-start(bf16[1,32,128,2,128]{2,1,3,0,4:T(8,128)(2,1)} %copy.38) | copy-start | bytes 6291460
